TPU v7x, 1024 devices: a whole 4x8x16 slice. The times are simulated.
1024 devices in a mesh: dp: 32 (over x_lo, z), tensor: 32 (over x_hi, y, core).
Axes of the slice: x: 4 (x_hi: 2, x_lo: 2; x = x_hi * 2 + x_lo), y: 8, z: 16, core: 2. Of those that a mesh axis runs over, the one named last changes fastest.
Arguments:
- queries: bfloat16 [32, 133, 4096], P('dp', None, 'tensor'), may hold values from -50 to 50
- keys: bfloat16 [32, 1024, 4096], P('dp', None, 'tensor'), may hold values from -4 to 4
- values: bfloat16 [32, 1024, 4096], P('dp', None, 'tensor'), may hold values from -6 to 6
- conv_kernel: float32 [32, 6, 11], P('tensor'), may hold values from -0.9 to 1.9
- span_start: int32 [32], P('dp'), may hold values from 0 to 896, as said below
- out_grad: bfloat16 [32, 128, 4096], P('dp', None, 'tensor'), may hold values from -6 to 6
- proj_weight: float32 [4096, 4096], P('tensor', 'dp'), may hold values from -0.09375 to 0.09375
- moment_one: float32 [4096, 4096], P('tensor', 'dp'), may hold values from -12 to 12
- moment_two: float32 [4096, 4096], P('tensor', 'dp'), may hold values from 1 to 100
Outputs:
- query_grad: bfloat16 [32, 133, 4096], P('dp', None, 'tensor')
- key_grad: bfloat16 [32, 1024, 4096], P('dp', None, 'tensor')
- value_grad: bfloat16 [32, 1024, 4096], P('dp', None, 'tensor')
- kernel_grad: float32 [32, 6, 11], P('tensor')
- proj_new: float32 [4096, 4096], P('tensor', 'dp')
- moment_one_new: float32 [4096, 4096], P('tensor', 'dp')
- moment_two_new: float32 [4096, 4096], P('tensor', 'dp')
Inputs may be any that keep to these rules, and one draw needn't show every extreme that they name: `span_start`: each sequence's first block row; one sequence starts at 0 and one at 896.
All inputs are finite; a program needn't handle non-finite values.
Results may differ from a plain program's by a relative error of at most 0.0029.
The roundings to bfloat16 on the way count: a program that leaves them out, or rounds other values in their place, can miss the bound.
Values may be sent and summed in bfloat16 or wider, within the bound.
A program may use at most 32 MiB of HBM per device.

v0:
```python
import math

import jax
import jax.numpy as jnp
from jax import lax
from jax.sharding import PartitionSpec as P

beta_one = 0.9
beta_two = 0.95
learn_rate = 0.01
decay_rate = 0.1
adam_eps = 1e-08
bias_one = 1.0 - 0.9**10
bias_two = 1.0 - 0.95**10


def contract_rows(left, right):
    return lax.dot_general(
        left, right, (((0,), (0,)), ((), ())), preferred_element_type=jnp.float32
    )


def contract_cols(left, right):
    return lax.dot_general(
        left, right, (((1,), (1,)), ((), ())), preferred_element_type=jnp.float32
    )


def shards(
    queries, keys, values, conv_kernel, span_start, out_grad, proj_weight, moment_one, moment_two
):
    first_pos = span_start[0]
    query_rows = queries[0]
    key_rows = keys[0]
    value_rows = values[0]
    kernel = conv_kernel[0]
    conv_rows, conv_cols = kernel.shape
    half_width = (conv_cols - 1) // 2
    span_len = out_grad.shape[1]
    key_count = key_rows.shape[0]
    query_count = query_rows.shape[0]
    head_dim = query_rows.shape[1]
    group_count = lax.axis_size("dp")
    score_scale = 1.0 / math.sqrt(head_dim)
    key_pos = jnp.arange(key_count, dtype=jnp.int32)
    row_pos = first_pos - (conv_rows - 1) + jnp.arange(query_count, dtype=jnp.int32)
    visible = key_pos[None, :] <= row_pos[:, None]
    masked = jnp.where(visible, contract_cols(query_rows, key_rows) * score_scale, 0.0)
    padded = jnp.pad(masked, ((0, 0), (half_width, half_width)))
    mixed_scores = jnp.zeros((span_len, key_count), jnp.float32)
    for tap_row in range(conv_rows):
        for tap_col in range(conv_cols):
            row_first = conv_rows - 1 - tap_row
            mixed_scores = (
                mixed_scores
                + kernel[tap_row, tap_col]
                * padded[row_first : row_first + span_len, tap_col : tap_col + key_count]
            )
    live_mask = visible[conv_rows - 1 :]
    row_top = jnp.max(jnp.where(live_mask, mixed_scores, -jnp.inf), axis=1, keepdims=True)
    exp_terms = jnp.where(live_mask, jnp.exp(mixed_scores - row_top), 0.0)
    weights_soft = exp_terms / jnp.sum(exp_terms, axis=1, keepdims=True)
    weights_bf = weights_soft.astype(jnp.bfloat16)
    attended = jnp.dot(weights_bf, value_rows, preferred_element_type=jnp.float32).astype(
        jnp.bfloat16
    )
    proj_bf = proj_weight.astype(jnp.bfloat16)
    local_grad = out_grad[0]
    upstream = lax.all_gather(local_grad, "tensor", axis=1, tiled=True)
    columns = upstream
    grad_out32 = contract_cols(columns, lax.all_gather(proj_bf, "dp", axis=1, tiled=True))
    grad_out = grad_out32.astype(jnp.bfloat16)
    grad_values = contract_rows(weights_bf, grad_out).astype(jnp.bfloat16)
    grad_weights = contract_cols(grad_out, value_rows)
    row_inner = jnp.sum(weights_soft * grad_weights, axis=1, keepdims=True)
    grad_mixed = weights_soft * (grad_weights - row_inner)
    grad_pad = jnp.pad(grad_mixed, ((conv_rows - 1, conv_rows - 1), (half_width, half_width)))
    grad_masked = jnp.zeros((query_count, key_count), jnp.float32)
    kernel_terms = []
    for tap_row in range(conv_rows):
        for tap_col in range(conv_cols):
            col_first = 2 * half_width - tap_col
            grad_masked = (
                grad_masked
                + kernel[tap_row, tap_col]
                * grad_pad[tap_row : tap_row + query_count, col_first : col_first + key_count]
            )
            row_first = conv_rows - 1 - tap_row
            kernel_terms.append(
                jnp.sum(
                    grad_mixed
                    * padded[row_first : row_first + span_len, tap_col : tap_col + key_count]
                )
            )
    kernel_local = jnp.stack(kernel_terms).reshape(conv_rows, conv_cols)
    grad_scores = jnp.where(visible, grad_masked, 0.0).astype(jnp.bfloat16)
    grad_query = (
        score_scale * jnp.dot(grad_scores, key_rows, preferred_element_type=jnp.float32)
    ).astype(jnp.bfloat16)
    grad_keys = (score_scale * contract_rows(grad_scores, query_rows)).astype(jnp.bfloat16)
    columns = upstream
    proj_sum = lax.psum_scatter(
        contract_rows(columns, attended), "dp", scatter_dimension=0, tiled=True
    ).T
    grad_proj = proj_sum / float(group_count)
    kernel_total = lax.psum(kernel_local, "dp") / float(group_count * span_len)
    moment_one_new = beta_one * moment_one + (1.0 - beta_one) * grad_proj
    moment_two_new = beta_two * moment_two + (1.0 - beta_two) * grad_proj * grad_proj
    first_hat = moment_one_new / bias_one
    second_hat = moment_two_new / bias_two
    proj_new = proj_weight - learn_rate * (
        first_hat / (jnp.sqrt(second_hat) + adam_eps) + decay_rate * proj_weight
    )
    return (
        grad_query[None],
        grad_keys[None],
        grad_values[None],
        kernel_total[None],
        proj_new,
        moment_one_new,
        moment_two_new,
    )


def solution(mesh):
    placed = (
        P("dp", None, "tensor"),
        P("dp", None, "tensor"),
        P("dp", None, "tensor"),
        P("tensor", None, None),
        P("dp"),
        P("dp", None, "tensor"),
        P("tensor", "dp"),
        P("tensor", "dp"),
        P("tensor", "dp"),
    )
    return jax.shard_map(
        shards,
        mesh=mesh,
        in_specs=placed,
        out_specs=(
            P("dp", None, "tensor"),
            P("dp", None, "tensor"),
            P("dp", None, "tensor"),
            P("tensor", None, None),
            P("tensor", "dp"),
            P("tensor", "dp"),
            P("tensor", "dp"),
        ),
        check_vma=False,
    )
```

profile of v0, /device:TPU:6, one launch (start us, length us, event | category | flops | bytes accessed | tf_op | source)
XLA Modules:
  0.0 420.5 jit_solution(15119157652295022297)
XLA Ops:
  7.2 0.7 all-gather.6.cloned.1.call-update
  8.0 1.5 convert_element_type.28
  9.4 0.0 reduce-scatter.2.cloned.1.call-start
  10.1 0.7 copy.19
  10.8 0.7 fusion.156
  11.5 0.7 fusion.155
  12.2 0.7 fusion.154
  13.0 0.7 fusion.153
  13.7 0.1 iota_compare_fusion
  13.8 1.3 fusion
  15.1 50.2 %select_reduce_fusion = (f32[128]{0:T(128)S(1)}, f32[128,1024]{1,0:T(8,128)S(1)}) fusion(pred[133,1024]{1,0:T(8,128)(4,1)S(1)} %iota_compare_fusion, f32[]{:T(128)} %bitcast.68, f32[]{:T(128)} %bitcast.67, f32[]{:T(128)} %bitcast.66, f32[]{:T(128)} %bitcast.65, f32[]{:T(128)} %bitcast.64, f32[133,1024]{1,0:T(8,128)S(1)} %fusion, f32[]{:T(128)} %bitcast.63, ...), kind=kLoop, calls=%fused_computation.283 | loop fusion | flops 17432448 | bytes 4358920 | tf_op jit(solution)/shard_map/reduce_max | solution.py:60
  65.3 0.3 fusion.140
  65.6 41.0 %all-gather.6.cloned.1.call-done = bf16[1,128,4096]{2,1,0:T(8,128)(2,1)} async-done(((bf16[1,128,128]{2,1,0:T(8,128)(2,1)}), bf16[1,128,4096]{2,1,0:T(8,128)(2,1)}) %all-gather.6.cloned.1.call-update) | async-done | bytes 1048592 | tf_op jit(solution)/shard_map/all_gather | solution.py:69
  106.6 127.1 %all-gather.4.cloned.1.call-done = bf16[128,4096]{1,0:T(8,128)(2,1)} async-done(((bf16[128,128]{1,0:T(8,128)(2,1)}), bf16[128,4096]{1,0:T(8,128)(2,1)}) %all-gather.4.cloned.1.call-update) | async-done | bytes 1048592 | tf_op jit(solution)/shard_map/all_gather | solution.py:71
  233.7 2.0 convolution_convert_fusion.1
  235.7 1.1 multiply_reduce_fusion.66
  236.8 0.1 copy-done.1
  236.9 2.0 convolution_bitcast_fusion
  239.0 1.0 copy-done.3
  240.0 3.1 multiply_reduce_fusion
  243.1 2.2 multiply_reduce_fusion.54
  245.3 3.2 multiply_reduce_fusion.18
  248.5 3.0 multiply_reduce_fusion.36
  251.5 42.4 %stack.267 = f32[66]{0:T(128)S(1)} concatenate(f32[1]{0:T(128)} %bitcast.74, f32[1]{0:T(128)} %bitcast.75, f32[1]{0:T(128)} %bitcast.76, f32[1]{0:T(128)} %bitcast.77, f32[1]{0:T(128)} %bitcast.78, f32[1]{0:T(128)} %bitcast.79, f32[1]{0:T(128)} %bitcast.80, f32[1]{0:T(128)} %bitcast.81, f32[1]{0:T(128)} %bitcast.82, f32[1]{0:T(128)} %bitcast.83, f32[1]{0:T(128)} %bitcast.84, ...), dimensions={0} | concatenate | bytes 528 | tf_op jit(solution)/shard_map/stack | solution.py:95
  294.0 0.1 reshape.26
  294.0 63.0 %psum.7 = f32[6,11]{1,0:T(8,128)S(1)} all-reduce(f32[6,11]{1,0:T(8,128)S(1)} %reshape.26), channel_id=1, replica_groups=mesh['dp'=32,'tensor'=32] {'dp'}, use_global_device_ids=true, to_apply=%region_69.70 | all-reduce | flops 66 | bytes 528 | tf_op jit(solution)/shard_map/psum | solution.py:106
  357.1 0.6 copy.16
  357.7 51.8 %select_convert_fusion = bf16[133,1024]{1,0:T(8,128)(2,1)S(1)} fusion(f32[128,1024]{1,0:T(8,128)S(1)} %get-tuple-element.83, f32[]{:T(128)} %bitcast.68, f32[]{:T(128)} %bitcast.67, f32[]{:T(128)} %bitcast.66, f32[]{:T(128)} %bitcast.65, f32[]{:T(128)} %bitcast.64, f32[]{:T(128)} %bitcast.63, f32[]{:T(128)} %bitcast.62, f32[]{:T(128)} %bitcast.61, ...), kind=kLoop, calls=%fused_computation.212 | loop fusion | flops 18249728 | bytes 797468 | tf_op jit(solution)/shard_map/convert_element_type | solution.py:96
  409.5 1.1 fusion.3
  410.6 1.0 fusion.2
  411.6 0.8 fusion.5
  412.4 1.5 multiply_subtract_fusion
  (21 shorter events, 0.1 us)
Async XLA Ops:
  7.2 228.5 %copy-start = (bf16[1,1024,128]{2,1,0:T(8,128)(2,1)S(1)}, bf16[1,1024,128]{2,1,0:T(8,128)(2,1)}, u32[]{:S(2)}) copy-start(bf16[1,1024,128]{2,1,0:T(8,128)(2,1)} %param.11) | copy-start | bytes 786436
  7.2 99.4 %all-gather.6.cloned.1.call-start = ((), (), s32[]{:S(2)}) async-start(), calls=%async_computation.3 | async-start | bytes 1081344 | tf_op jit(solution)/shard_map/all_gather | solution.py:69
  7.9 225.8 %all-gather.4.cloned.1.call-start = ((), (), s32[]{:S(2)}) async-start(), calls=%async_computation.1 | async-start | bytes 1081344 | tf_op jit(solution)/shard_map/all_gather | solution.py:71
  9.4 403.0 %reduce-scatter.2.cloned.1.call-start = ((), (), s32[]{:S(2)}) async-start(), calls=%async_computation.2 | async-start | bytes 2162688 | tf_op jit(solution)/shard_map/reduce_scatter | solution.py:102
  235.7 1.2 copy-start.1
  238.9 1.0 copy-start.3
  245.3 164.2 %copy-start.5 = (bf16[1,133,128]{2,1,0:T(8,128)(2,1)S(1)}, bf16[1,133,128]{2,1,0:T(8,128)(2,1)}, u32[]{:S(2)}) copy-start(bf16[1,133,128]{2,1,0:T(8,128)(2,1)} %param.9) | copy-start | bytes 102148
  248.5 163.1 %copy-start.2 = (bf16[1,1024,128]{2,1,0:T(8,128)(2,1)S(1)}, bf16[1,1024,128]{2,1,0:T(8,128)(2,1)}, u32[]{:S(2)}) copy-start(bf16[1,1024,128]{2,1,0:T(8,128)(2,1)} %param.10) | copy-start | bytes 786436
  251.5 160.9 %copy-start.4 = (f32[128,128]{1,0:T(8,128)S(1)}, f32[128,128]{1,0:T(8,128)}, u32[]{:S(2)}) copy-start(f32[128,128]{1,0:T(8,128)} %param.15) | copy-start | bytes 196612
  251.5 160.9 %copy-start.6 = (f32[128,128]{1,0:T(8,128)S(1)}, f32[128,128]{1,0:T(8,128)}, u32[]{:S(2)}) copy-start(f32[128,128]{1,0:T(8,128)} %param.16) | copy-start | bytes 196612
  251.5 160.9 %copy-start.7 = (f32[128,128]{1,0:T(8,128)S(1)}, f32[128,128]{1,0:T(8,128)}, u32[]{:S(2)}) copy-start(f32[128,128]{1,0:T(8,128)} %param.17) | copy-start | bytes 196612
Sparse Core Ops, SparseCore 0:
  12.3 94.2 all-gather.5
  109.8 123.8 all-gather.3
  239.1 139.8 reduce-scatter.1
where the time goes:
time: 423 us; the launch traced here: 421 us
  waiting for transfers between devices  169 us (40%)
  other arithmetic  117 us (28%)
  blocking collectives  63 us (15%)
  local copies, waits for them, and re-layouts  47.8 us (11%)
  between operations  14.5 us (3%)
  matrix products  9.25 us (2%)
    all_gather x1, waiting for transfers between devices, shards(): lax.all_gather(proj_bf, 'dp', axis=1, tiled=True)  127 us
    psum x1, blocking collectives, shards(): kernel_total = lax.psum(kernel_local, 'dp') / float(group_count * span_len)  63 us
    convert_element_type x1, other arithmetic, shards(): grad_scores = jnp.where(visible, grad_masked, 0.0).astype(jnp.bfloat16)  51.8 us
    reduce_max x1, other arithmetic, shards(): jnp.max(jnp.where(live_mask, mixed_scores, -jnp.inf), axis=1, keepdims=True)  50.2 us
    another operation x1, local copies, waits for them, and re-layouts, shards(): kernel_local = jnp.stack(kernel_terms).reshape(conv_rows, conv_cols)  42.4 us
    all_gather x1, waiting for transfers between devices, shards(): upstream = lax.all_gather(local_grad, 'tensor', axis=1, tiled=True)  41 us
    reduce_sum x4, other arithmetic, shards(): jnp.sum(grad_mixed * padded[row_first:row_first + span_len, tap_col:tap_c...  11.6 us
  transfers between devices with their start and end apart: 3, of which 2 were waited for; matrix products, arithmetic and copies ran while one was open for 40% of the time, Pallas kernels for 0%

commit v1 on v0

v1 whole, which is shorter than its diff:
```python
import functools
import math

import jax
import jax.numpy as jnp
from jax import lax
from jax.experimental import pallas as pl
from jax.experimental.pallas import tpu as pltpu
from jax.sharding import PartitionSpec as P

beta_one = 0.9
beta_two = 0.95
learn_rate = 0.01
decay_rate = 0.1
adam_eps = 1e-08
bias_one = 1.0 - 0.9**10
bias_two = 1.0 - 0.95**10

MESH = pl.DeviceIdType.MESH
F32 = jnp.float32
BF16 = jnp.bfloat16
NX, NZ, NY = 2, 16, 8
STEP_Z, STEP_Y = 2, 1
CR, CC = 6, 11
HALF = 5
TILE = 32


def dot_cols(left, right):
    return lax.dot_general(
        left, right, (((1,), (1,)), ((), ())), preferred_element_type=F32
    )


def dot_rows(left, right):
    return lax.dot_general(
        left, right, (((0,), (0,)), ((), ())), preferred_element_type=F32
    )


def dot_mid(left, right):
    return lax.dot_general(
        left, right, (((1,), (0,)), ((), ())), preferred_element_type=F32
    )


def kernel(
    q_ref, k_ref, v_ref, tap_ref, start_ref, og_ref, w_ref, m1_ref, m2_ref,
    dq_ref, dk_ref, dv_ref, kg_ref, wn_ref, m1n_ref, m2n_ref,
    w_all, o_all, u_all, t_all, xp, prob, prob_bf, dcp, ds, qp, taps, acc, kg_all, dpp,
    do_bf,
    w_send, w_recv, o_send, o_recv, u_send, u_recv, t_send, t_recv, p_send, kg_send, kg_recv,
):
    d = lax.axis_index("dp")
    t = lax.axis_index("tensor")
    dp_count = NX * NZ
    z, xl = lax.rem(d, NZ), d // NZ
    core, yy = lax.rem(t, 2), lax.rem(t // 2, NY)
    xh = t // (2 * NY)
    scale = 1.0 / math.sqrt(k_ref.shape[2])
    blocks = k_ref.shape[1] // 128

    def dp_at(x, zz):
        return x * NZ + lax.rem(zz + 2 * NZ, NZ)

    def tn_at(x, y, c):
        return (x * NY + lax.rem(y + 2 * NY, NY)) * 2 + c

    pending = []

    def push(buf, index, sends, slot, recvs, target):
        copy = pltpu.make_async_remote_copy(
            src_ref=buf.at[index], dst_ref=buf.at[index],
            send_sem=sends.at[slot], recv_sem=recvs.at[index],
            device_id=target, device_id_type=MESH,
        )
        copy.start()
        pending.append(copy)

    def arrive(buf, index, recvs):
        pltpu.make_async_remote_copy(
            src_ref=buf.at[index], dst_ref=buf.at[index],
            send_sem=p_send.at[0], recv_sem=recvs.at[index],
            device_id=(d, t), device_id_type=MESH,
        ).wait_recv()

    up, down = NZ // 2, NZ - 1 - NZ // 2

    class GatherDp:
        def __init__(self, buf, sends, recvs):
            self.buf, self.sends, self.recvs, self.slot = buf, sends, recvs, 0

        def push(self, index, target):
            push(self.buf, index, self.sends, self.slot, self.recvs, target)
            self.slot += 1

        def ring(self, at):
            for q in range(1, STEP_Z + 1):
                if at + q <= up:
                    self.push(dp_at(xl, z - at), (dp_at(xl, z + q), t))
                if at + q <= down:
                    self.push(dp_at(xl, z + at), (dp_at(xl, z - q), t))

        def cross(self, offset):
            self.push(dp_at(xl, z + offset), (dp_at(1 - xl, z), t))

        def begin(self):
            self.ring(0)
            self.cross(0)

        def stage(self, number):
            first = number * STEP_Z
            near = []
            for q in range(STEP_Z, 0, -1):
                for sign, limit in ((-1, up), (1, down)):
                    if first + q <= limit:
                        arrive(self.buf, dp_at(xl, z + sign * (first + q)), self.recvs)
                        near.append(sign * (first + q))
                if q == STEP_Z:
                    self.ring(first + q)
            for offset in near:
                self.cross(offset)

        stages = -(-up // STEP_Z)

        def finish(self):
            for other in range(NZ):
                arrive(self.buf, dp_at(1 - xl, z + other), self.recvs)

    y_up, y_down = NY // 2, NY - 1 - NY // 2

    class GatherTn:
        def __init__(self, buf, sends, recvs):
            self.buf, self.sends, self.recvs, self.slot = buf, sends, recvs, 0

        def push(self, index, target):
            push(self.buf, index, self.sends, self.slot, self.recvs, target)
            self.slot += 1

        def ring(self, x, at):
            for q in range(1, STEP_Y + 1):
                if at + q <= y_up:
                    self.push(tn_at(x, yy - at, core), (d, tn_at(xh, yy + q, core)))
                if at + q <= y_down:
                    self.push(tn_at(x, yy + at, core), (d, tn_at(xh, yy - q, core)))

        def mate(self, x, offset):
            self.push(tn_at(x, yy + offset, core), (d, tn_at(xh, yy, 1 - core)))

        def begin(self):
            self.push(t, (d, tn_at(1 - xh, yy, core)))
            self.ring(xh, 0)
            self.mate(xh, 0)

        def crossed(self):
            arrive(self.buf, tn_at(1 - xh, yy, core), self.recvs)
            self.ring(1 - xh, 0)
            self.mate(1 - xh, 0)

        def stage(self, number, x):
            first = number * STEP_Y
            near = []
            for q in range(STEP_Y, 0, -1):
                for sign, limit in ((-1, y_up), (1, y_down)):
                    if first + q <= limit:
                        arrive(self.buf, tn_at(x, yy + sign * (first + q), core), self.recvs)
                        near.append(sign * (first + q))
                if q == STEP_Y:
                    self.ring(x, first + q)
            for offset in near:
                self.mate(x, offset)

        stages = -(-y_up // STEP_Y)

        def both(self, number):
            self.stage(number, xh)
            self.stage(number, 1 - xh)

        def finish(self):
            for x in range(2):
                for other in range(NY):
                    arrive(self.buf, tn_at(x, yy + other, 1 - core), self.recvs)

    gw = GatherDp(w_all, w_send, w_recv)
    go = GatherDp(o_all, o_send, o_recv)
    gu = GatherTn(u_all, u_send, u_recv)
    gt = GatherTn(t_all, t_send, t_recv)

    w_all[d] = w_ref[...].astype(BF16)
    u_all[t] = og_ref[0]

    targets = [(dp_at(1 - xl, z), t), (d, tn_at(1 - xh, yy, core)), (d, tn_at(xh, yy, 1 - core))]
    for q in range(1, STEP_Z + 1):
        targets += [(dp_at(xl, z + q), t), (dp_at(xl, z - q), t)]
    for q in range(1, STEP_Y + 1):
        targets += [(d, tn_at(xh, yy + q, core)), (d, tn_at(xh, yy - q, core))]
    barrier = pltpu.get_barrier_semaphore()
    for target in targets:
        pl.semaphore_signal(barrier, inc=1, device_id=target, device_id_type=MESH)
    pl.semaphore_signal(barrier, inc=1, device_id=(t, d), device_id_type=MESH)

    qp[pl.ds(128, 16), :] = jnp.zeros((16, 128), BF16)
    qp[pl.ds(0, q_ref.shape[1]), :] = q_ref[0]
    for edge in (0, blocks + 1):
        xp[edge] = jnp.zeros((xp.shape[1], 128), F32)
        dcp[edge] = jnp.zeros((dcp.shape[1], 128), F32)
    for inner in range(1, blocks + 1):
        dcp[inner, pl.ds(0, 8), :] = jnp.zeros((8, 128), F32)
        dcp[inner, pl.ds(136, 16), :] = jnp.zeros((16, 128), F32)
    for a in range(CR):
        for b in range(CC):
            taps[a * CC + b] = jnp.full((8, 128), tap_ref[0, a, b], F32)
    acc[...] = jnp.zeros(acc.shape, F32)

    pl.semaphore_wait(barrier, len(targets) + 1)

    gw.begin()
    gu.begin()

    transpose = pltpu.make_async_remote_copy(
        src_ref=u_all.at[t], dst_ref=t_all.at[d],
        send_sem=p_send.at[0], recv_sem=t_recv.at[d],
        device_id=(t, d), device_id_type=MESH,
    )

    @pl.when(d != t)
    def _():
        transpose.start()

    @pl.when(d == t)
    def _():
        t_all[t] = og_ref[0]

    start = start_ref[0]

    def lanes(rows):
        return lax.broadcasted_iota(jnp.int32, (rows, 128), 1)

    def sublanes(rows):
        return lax.broadcasted_iota(jnp.int32, (rows, 128), 0)

    def visible(jb, rows, first):
        return jb * 128 + lanes(rows) <= start + (first + sublanes(rows))

    def shifted(prev, cur, nxt, by):
        if by == 0:
            return cur
        lane = lanes(cur.shape[0])
        if by > 0:
            return pltpu.roll(jnp.where(lane >= by, cur, nxt), 128 - by, 1)
        return pltpu.roll(jnp.where(lane < 128 + by, cur, prev), -by, 1)

    def score_block(jb, carry):
        keys = k_ref[0, pl.ds(pl.multiple_of(jb * 128, 128), 128), :]
        raw = dot_cols(qp[...], keys) * scale
        xp[jb + 1] = jnp.where(visible(jb, xp.shape[1], -HALF), raw, 0.0)
        return carry

    lax.fori_loop(0, blocks, score_block, 0)

    def row_sums(src, jb, first, rows, flip):
        prev = src[jb, pl.ds(first, rows), :]
        cur = src[jb + 1, pl.ds(first, rows), :]
        nxt = src[jb + 2, pl.ds(first, rows), :]
        sums = [None] * CR
        for b in range(CC):
            moved = shifted(prev, cur, nxt, (HALF - b) if flip else (b - HALF))
            moved = moved.reshape(rows // 8, 8, 128)
            for a in range(CR):
                term = taps[a * CC + b][None] * moved
                sums[a] = term if b == 0 else sums[a] + term
        return [s.reshape(rows, 128) for s in sums]

    def forward_tile(tile):
        first = tile * TILE
        rows = TILE + 8

        def mix(jb, top):
            sums = row_sums(xp, jb, first, rows, False)
            total = sums[CR - 1]
            for a in range(CR - 1):
                total = total + pltpu.roll(sums[a], rows - (HALF - a), 0)
            total = jnp.where(visible(jb, TILE, first), total[:TILE], -jnp.inf)
            prob[jb, pl.ds(first, TILE), :] = total
            return jnp.maximum(top, total)

        top = lax.fori_loop(0, blocks, mix, jnp.full((TILE, 128), -jnp.inf, F32))
        top = jnp.max(top, axis=1, keepdims=True)

        total = jnp.zeros((TILE, 128), F32)
        for jb in range(blocks):
            term = jnp.exp(prob[jb, pl.ds(first, TILE), :] - top)
            prob[jb, pl.ds(first, TILE), :] = term
            total = total + term
        inverse = 1.0 / jnp.sum(total, axis=1, keepdims=True)
        out = jnp.zeros((TILE, 128), F32)
        for jb in range(blocks):
            weight = prob[jb, pl.ds(first, TILE), :] * inverse
            prob[jb, pl.ds(first, TILE), :] = weight
            rounded = weight.astype(BF16)
            prob_bf[jb, pl.ds(first, TILE), :] = rounded
            out = out + dot_mid(rounded, v_ref[0, pl.ds(jb * 128, 128), :])
        o_all[d, pl.ds(first, TILE), :] = out.astype(BF16)

    forward_tile(0)
    gu.crossed()
    gw.stage(0)
    gu.stage(0, xh)
    forward_tile(1)
    gu.stage(0, 1 - xh)
    gu.stage(1, xh)

    @pl.when(d != t)
    def _():
        pltpu.make_async_remote_copy(
            src_ref=u_all.at[t], dst_ref=t_all.at[t],
            send_sem=p_send.at[0], recv_sem=t_recv.at[t],
            device_id=(t, d), device_id_type=MESH,
        ).wait_recv()

    gt.begin()
    forward_tile(2)
    gw.stage(1)
    gu.stage(1, 1 - xh)
    gu.stage(2, xh)
    forward_tile(3)
    gw.stage(2)
    go.begin()
    gu.stage(2, 1 - xh)
    gu.stage(3, xh)
    gt.crossed()
    gt.stage(0, xh)
    gu.stage(3, 1 - xh)
    gt.stage(0, 1 - xh)
    gw.stage(3)
    go.stage(0)
    gt.both(1)
    gu.finish()
    gw.finish()

    grad_out = jnp.zeros((128, 128), F32)
    for c in range(dp_count // 2):
        left = jnp.concatenate([u_all[2 * c], u_all[2 * c + 1]], axis=1)
        right = jnp.concatenate([w_all[2 * c], w_all[2 * c + 1]], axis=1)
        grad_out = grad_out + dot_cols(left, right)
    do_bf[...] = grad_out.astype(BF16)

    inner = jnp.zeros((128, 128), F32)
    for jb in range(blocks):
        part = dot_cols(do_bf[...], v_ref[0, pl.ds(jb * 128, 128), :])
        dpp[jb] = part
        inner = inner + prob[jb] * part
    inner = jnp.sum(inner, axis=1, keepdims=True)
    for jb in range(blocks):
        dcp[jb + 1, pl.ds(8, 128), :] = prob[jb] * (dpp[jb] - inner)

    def tap_grads(tile):
        first = tile * TILE
        rows = TILE + 8

        def body(jb, carry):
            wide = xp[jb + 1, pl.ds(first, rows), :]
            scores = []
            for a in range(CR):
                turned = wide if a == CR - 1 else pltpu.roll(wide, rows - (HALF - a), 0)
                scores.append(turned[:TILE].reshape(TILE // 8, 8, 128))
            prev = dcp[jb, pl.ds(8 + first, TILE), :]
            cur = dcp[jb + 1, pl.ds(8 + first, TILE), :]
            nxt = dcp[jb + 2, pl.ds(8 + first, TILE), :]
            for b in range(CC):
                moved = shifted(prev, cur, nxt, HALF - b).reshape(TILE // 8, 8, 128)
                for a in range(CR):
                    acc[a * 16 + b] += jnp.sum(scores[a] * moved, axis=0)
            return carry

        lax.fori_loop(0, blocks, body, 0)

    def grad_tile(first, count):
        rows = count + 8

        def body(jb, carry):
            sums = row_sums(dcp, jb, first, rows, True)
            total = None
            for a in range(CR):
                turned = pltpu.roll(sums[a], rows - (3 + a), 0)[:count]
                total = turned if total is None else total + turned
            total = jnp.where(visible(jb, count, first - HALF), total, 0.0)
            ds[jb, pl.ds(first, count), :] = total.astype(BF16)
            return carry

        lax.fori_loop(0, blocks, body, 0)

    tap_grads(0)
    tap_grads(1)
    go.stage(1)
    gt.both(2)
    tap_grads(2)
    tap_grads(3)

    folded = jnp.sum(acc[...], axis=1)
    kg_row = lax.dot_general(
        jnp.ones((8, 128), F32), folded, (((1,), (1,)), ((), ())),
        preferred_element_type=F32, precision=lax.Precision.HIGHEST,
    )
    kg_all[d] = kg_row[0:1]
    go.stage(2)
    gt.both(3)
    for r in range(1, dp_count):
        push(kg_all, d, kg_send, r, kg_recv, (lax.rem(d + r, dp_count), t))

    grad_tile(0, TILE)
    grad_tile(TILE, TILE)
    go.stage(3)
    grad_tile(2 * TILE, TILE)
    grad_tile(3 * TILE, TILE)
    grad_tile(4 * TILE, 16)

    grad_query = jnp.zeros((qp.shape[0], 128), F32)
    for jb in range(blocks):
        span = pl.ds(jb * 128, 128)
        grad_query = grad_query + dot_mid(ds[jb], k_ref[0, span, :])
        dk_ref[0, span, :] = (scale * dot_rows(ds[jb], qp[...])).astype(BF16)
        dv_ref[0, span, :] = dot_rows(prob_bf[jb], do_bf[...]).astype(BF16)
    dq_ref[0] = (scale * grad_query[: q_ref.shape[1]]).astype(BF16)

    gt.finish()
    go.finish()
    total = jnp.zeros((128, 128), F32)
    for g in range(dp_count // 2):
        left = jnp.concatenate([o_all[2 * g], o_all[2 * g + 1]], axis=0)
        right = jnp.concatenate([t_all[2 * g], t_all[2 * g + 1]], axis=0)
        total = total + dot_rows(left, right)
    grad = total * (1.0 / dp_count)
    one = beta_one * m1_ref[...] + (1.0 - beta_one) * grad
    two = beta_two * m2_ref[...] + (1.0 - beta_two) * grad * grad
    m1n_ref[...] = one
    m2n_ref[...] = two
    wn_ref[...] = w_ref[...] - learn_rate * (
        (one / bias_one) / (jnp.sqrt(two / bias_two) + adam_eps) + decay_rate * w_ref[...]
    )

    for r in range(1, dp_count):
        arrive(kg_all, lax.rem(d + r, dp_count), kg_recv)
    kg_sum = kg_all[0]
    for r in range(1, dp_count):
        kg_sum = kg_sum + kg_all[r]
    kg_sum = kg_sum * (1.0 / (dp_count * 128))
    for a in range(CR):
        row = kg_sum if a == 0 else pltpu.roll(kg_sum, 128 - 16 * a, 1)
        kg_ref[0, pl.ds(a, 1), :] = row[:, :CC]

    for copy in pending:
        copy.wait_send()

    @pl.when(d != t)
    def _():
        transpose.wait_send()


def shards(*args):
    queries, keys = args[0], args[1]
    proj = args[6]
    vmem = pl.BlockSpec(memory_space=pltpu.VMEM)
    smem = pl.BlockSpec(memory_space=pltpu.SMEM)
    dma = pltpu.SemaphoreType.DMA
    outs = (
        jax.ShapeDtypeStruct(queries.shape, BF16),
        jax.ShapeDtypeStruct(keys.shape, BF16),
        jax.ShapeDtypeStruct(keys.shape, BF16),
        jax.ShapeDtypeStruct(args[3].shape, F32),
        jax.ShapeDtypeStruct(proj.shape, F32),
        jax.ShapeDtypeStruct(proj.shape, F32),
        jax.ShapeDtypeStruct(proj.shape, F32),
    )
    gathered = pltpu.VMEM((32, 128, 128), BF16)
    blocks = keys.shape[1] // 128
    return pl.pallas_call(
        kernel,
        out_shape=outs,
        in_specs=[vmem, vmem, vmem, smem, smem, vmem, vmem, vmem, vmem],
        out_specs=[vmem] * 7,
        scratch_shapes=[
            gathered, gathered, gathered, gathered,
            pltpu.VMEM((blocks + 2, 144, 128), F32),
            pltpu.VMEM((blocks, 128, 128), F32),
            pltpu.VMEM((blocks, 128, 128), BF16),
            pltpu.VMEM((blocks + 2, 152, 128), F32),
            pltpu.VMEM((blocks, 144, 128), BF16),
            pltpu.VMEM((144, 128), BF16),
            pltpu.VMEM((CR * CC, 8, 128), F32),
            pltpu.VMEM((128, 8, 128), F32),
            pltpu.VMEM((32, 1, 128), F32),
            pltpu.VMEM((blocks, 128, 128), F32),
            pltpu.VMEM((128, 128), BF16),
            dma((32,)), dma((32,)), dma((32,)), dma((32,)),
            dma((32,)), dma((32,)), dma((32,)), dma((32,)),
            dma((1,)), dma((32,)), dma((32,)),
        ],
        compiler_params=pltpu.CompilerParams(collective_id=0, has_side_effects=True),
    )(*args)


def solution(mesh):
    heads = P("dp", None, "tensor")
    taps = P("tensor", None, None)
    grid = P("tensor", "dp")
    return jax.shard_map(
        shards,
        mesh=mesh,
        in_specs=(heads, heads, heads, taps, P("dp"), heads, grid, grid, grid),
        out_specs=(heads, heads, heads, taps, grid, grid, grid),
        check_vma=False,
    )
```

time: 423 us -> 82.9 us (0.20)
  the two profiles are of different devices: /device:TPU:6 before, /device:TPU:28 now
where the time goes in v1:
time: 82.9 us; the launch traced here: 82.4 us
  Pallas kernels  72.3 us (87%)
  local copies, waits for them, and re-layouts  8.84 us (11%)
  between operations  1.3 us (2%)
    pallas_call x1, Pallas kernels, shards(): pl.pallas_call(kernel, out_shape=outs, in_specs=[vmem, vmem, vmem, smem,...  72.3 us
    unnamed x17, local copies, waits for them, and re-layouts  8.26 us

profile of v1, /device:TPU:28, one launch (start us, length us, event | category | flops | bytes accessed | tf_op | source)
XLA Modules:
  0.0 82.4 jit_solution(3725561652566411307)
XLA Ops:
  1.3 1.3 %copy.16.tap_ref = f32[1,6,11]{2,1,0:T(8,128)} copy(f32[1,6,11]{2,0,1:T(1,128)} %param.12) | data formatting | bytes 528 | tf_op args[3]
  2.6 72.3 %shard_map.144 = (bf16[1,133,128]{2,1,0:T(8,128)(2,1)}, bf16[1,1024,128]{2,1,0:T(8,128)(2,1)}, bf16[1,1024,128]{2,1,0:T(8,128)(2,1)}, f32[1,6,11]{2,1,0:T(8,128)...) custom-call(bf16[1,133,128]{2,1,0:T(8,128)(2,1)} %q_ref.1, bf16[1,1024,128]{2,1,0:T(8,128)(2,1)} %k_ref.1, ...), custom_call_target="tpu_custom_call" | custom-call | tf_op jit(solution)/shard_map/pallas_call | solution.py:477
  74.8 0.0 copy-start.4
  74.9 0.7 copy-done.4
  75.5 0.6 copy.17
  76.1 1.4 %copy.25 = bf16[1,133,128]{2,1,0:T(8,128)(2,1)} copy(bf16[1,133,128]{2,1,0:T(8,128)(2,1)} %get-tuple-element.21) | data formatting | bytes 68096
  77.5 0.0 copy-start
  77.5 1.7 %copy.26 = bf16[1,1024,128]{2,1,0:T(8,128)(2,1)} copy(bf16[1,1024,128]{2,1,0:T(8,128)(2,1)} %get-tuple-element.22) | data formatting | bytes 524288
  79.2 0.0 copy-done
  79.2 0.0 copy-start.3
  79.2 0.7 copy.27
  79.9 0.2 copy-done.3
  80.1 0.0 copy-start.2
  80.1 0.6 copy.28
  80.7 0.2 copy-done.2
  80.9 0.0 copy-start.1
  80.9 0.6 copy.29
  81.6 0.2 copy-done.1
  81.8 0.6 copy.30
Async XLA Ops:
  74.8 0.7 copy-start.4
  77.5 1.7 %copy-start = (bf16[1,1024,128]{2,1,0:T(8,128)(2,1)S(1)}, bf16[1,1024,128]{2,1,0:T(8,128)(2,1)}, u32[]{:S(2)}) copy-start(bf16[1,1024,128]{2,1,0:T(8,128)(2,1)} %get-tuple-element.23) | copy-start | bytes 786436
  79.2 0.9 %copy-start.3 = (f32[128,128]{1,0:T(8,128)S(1)}, f32[128,128]{1,0:T(8,128)}, u32[]{:S(2)}) copy-start(f32[128,128]{1,0:T(8,128)} %get-tuple-element.25) | copy-start | bytes 196612
  80.1 0.9 %copy-start.2 = (f32[128,128]{1,0:T(8,128)S(1)}, f32[128,128]{1,0:T(8,128)}, u32[]{:S(2)}) copy-start(f32[128,128]{1,0:T(8,128)} %get-tuple-element.26) | copy-start | bytes 196612
  80.9 0.9 %copy-start.1 = (f32[128,128]{1,0:T(8,128)S(1)}, f32[128,128]{1,0:T(8,128)}, u32[]{:S(2)}) copy-start(f32[128,128]{1,0:T(8,128)} %get-tuple-element.27) | copy-start | bytes 196612

commit v2 on v1

v2 whole, which is shorter than its diff:
```python
import functools
import math

import jax
import jax.numpy as jnp
from jax import lax
from jax.experimental import pallas as pl
from jax.experimental.pallas import tpu as pltpu
from jax.sharding import PartitionSpec as P

beta_one = 0.9
beta_two = 0.95
learn_rate = 0.01
decay_rate = 0.1
adam_eps = 1e-08
bias_one = 1.0 - 0.9**10
bias_two = 1.0 - 0.95**10

MESH = pl.DeviceIdType.MESH
F32 = jnp.float32
BF16 = jnp.bfloat16
NX, NZ, NY = 2, 16, 8
STEP_Z, STEP_Y = 2, 2
CR, CC = 6, 11
HALF = 5
TILE = 32
WIDE = 64


def dot_cols(left, right):
    return lax.dot_general(
        left, right, (((1,), (1,)), ((), ())), preferred_element_type=F32
    )


def dot_rows(left, right):
    return lax.dot_general(
        left, right, (((0,), (0,)), ((), ())), preferred_element_type=F32
    )


def dot_mid(left, right):
    return lax.dot_general(
        left, right, (((1,), (0,)), ((), ())), preferred_element_type=F32
    )


def kernel(
    q_hbm, k_hbm, v_hbm, tap_ref, start_ref, og_hbm, w_hbm, m1_hbm, m2_hbm,
    dq_ref, dk_ref, dv_ref, kg_ref, wn_ref, m1n_ref, m2n_ref,
    w_all, o_all, u_all, t_all, xp, prob, prob_bf, dcp, ds, qp, taps, acc, kg_all, dpp,
    do_bf, q_ref, k_ref, v_ref, w_ref, m1_ref, m2_ref, o_own, load_sem,
    w_send, w_recv, o_send, o_recv, u_send, u_recv, t_send, t_recv, p_send, kg_sem,
):
    d = lax.axis_index("dp")
    t = lax.axis_index("tensor")
    dp_count = NX * NZ
    z, xl = lax.rem(d, NZ), d // NZ
    core, yy = lax.rem(t, 2), lax.rem(t // 2, NY)
    xh = t // (2 * NY)
    scale = 1.0 / math.sqrt(k_ref.shape[2])
    blocks = k_ref.shape[1] // 128

    def dp_at(x, zz):
        return x * NZ + lax.rem(zz + 2 * NZ, NZ)

    def tn_at(x, y, c):
        return (x * NY + lax.rem(y + 2 * NY, NY)) * 2 + c

    def part_of(buf, index, piece, pieces):
        rows = buf.shape[1] // pieces
        return buf.at[index, pl.ds(piece * rows, rows)] if pieces > 1 else buf.at[index]

    def push(ref, send, recv, target):
        pltpu.make_async_remote_copy(
            src_ref=ref, dst_ref=ref, send_sem=send, recv_sem=recv,
            device_id=target, device_id_type=MESH,
        ).start()

    def landed(ref, send, recv):
        return pltpu.make_async_remote_copy(
            src_ref=ref, dst_ref=ref, send_sem=send, recv_sem=recv,
            device_id=(d, t), device_id_type=MESH,
        )

    up, down = NZ // 2, NZ - 1 - NZ // 2

    class GatherDp:
        def __init__(self, buf, sends, recvs, pieces):
            self.buf, self.sends, self.recvs, self.pieces = buf, sends, recvs, pieces

        def ring_sem(self, zz, piece):
            return self.recvs.at[lax.rem(zz + 2 * NZ, NZ) * self.pieces + piece]

        def ring(self, at, piece):
            for q in range(STEP_Z, 0, -1):
                for sign, limit in ((1, up), (-1, down)):
                    if at + q <= limit:
                        ref = part_of(self.buf, dp_at(xl, z - sign * at), piece, self.pieces)
                        push(ref, self.sends.at[0], self.ring_sem(z - sign * at, piece), (dp_at(xl, z + sign * q), t))

        def cross(self, offset, piece):
            ref = part_of(self.buf, dp_at(xl, z + offset), piece, self.pieces)
            push(ref, self.sends.at[0], self.recvs.at[NZ * self.pieces], (dp_at(1 - xl, z), t))

        def begin(self):
            for piece in range(self.pieces):
                self.ring(0, piece)
            for piece in range(self.pieces):
                self.cross(0, piece)

        def stage(self, number):
            first = number * STEP_Z
            for piece in range(self.pieces):
                near = []
                for q in range(STEP_Z, 0, -1):
                    for sign, limit in ((-1, up), (1, down)):
                        if first + q <= limit:
                            offset = sign * (first + q)
                            ref = part_of(self.buf, dp_at(xl, z + offset), piece, self.pieces)
                            landed(ref, self.sends.at[0], self.ring_sem(z + offset, piece)).wait_recv()
                            near.append(offset)
                    if q == STEP_Z:
                        self.ring(first + q, piece)
                for offset in near:
                    self.cross(offset, piece)

        stages = -(-up // STEP_Z)

        def finish(self):
            ref = self.buf.at[pl.ds((1 - xl) * NZ, NZ)]
            landed(ref, self.sends.at[0], self.recvs.at[NZ * self.pieces]).wait_recv()

        def drain(self):
            ref = self.buf.at[pl.ds(0, 2 * NZ - 1)]
            landed(ref, self.sends.at[0], self.recvs.at[0]).wait_send()

    y_up, y_down = NY // 2, NY - 1 - NY // 2

    def slot_of(x, y, c):
        return (c * 2 + x) * NY + lax.rem(y + 2 * NY, NY)

    class GatherTn:
        def __init__(self, buf, sends, recvs):
            self.buf, self.sends, self.recvs = buf, sends, recvs

        def push(self, x, y, sem, target):
            push(self.buf.at[slot_of(x, y, core)], self.sends.at[0], sem, target)

        def ring_sem(self, x, y):
            return self.recvs.at[slot_of(x, y, 0)]

        def ring(self, x, at):
            for q in range(STEP_Y, 0, -1):
                for sign, limit in ((1, y_up), (-1, y_down)):
                    if at + q <= limit:
                        self.push(x, yy - sign * at, self.ring_sem(x, yy - sign * at), (d, tn_at(xh, yy + sign * q, core)))

        def mate(self, x, offset):
            self.push(x, yy + offset, self.recvs.at[2 * NY], (d, tn_at(xh, yy, 1 - core)))

        def begin(self):
            self.push(xh, yy, self.ring_sem(xh, yy), (d, tn_at(1 - xh, yy, core)))
            self.ring(xh, 0)
            self.mate(xh, 0)

        def arrive(self, x, y):
            landed(self.buf.at[slot_of(x, y, core)], self.sends.at[0], self.ring_sem(x, y)).wait_recv()

        def crossed(self):
            self.arrive(1 - xh, yy)
            self.ring(1 - xh, 0)
            self.mate(1 - xh, 0)

        def stage(self, number, x):
            first = number * STEP_Y
            near = []
            for q in range(STEP_Y, 0, -1):
                for sign, limit in ((-1, y_up), (1, y_down)):
                    if first + q <= limit:
                        self.arrive(x, yy + sign * (first + q))
                        near.append(sign * (first + q))
                if q == STEP_Y:
                    self.ring(x, first + q)
            for offset in near:
                self.mate(x, offset)

        stages = -(-y_up // STEP_Y)

        def both(self, number):
            if number < self.stages:
                self.stage(number, xh)
                self.stage(number, 1 - xh)

        def finish(self):
            ref = self.buf.at[pl.ds((1 - core) * 2 * NY, 2 * NY)]
            landed(ref, self.sends.at[0], self.recvs.at[2 * NY]).wait_recv()

        def drain(self):
            ref = self.buf.at[pl.ds(0, 4 * NY - 1)]
            landed(ref, self.sends.at[0], self.recvs.at[0]).wait_send()

    gw = GatherDp(w_all, w_send, w_recv, 2)
    go = GatherDp(o_all, o_send, o_recv, 1)
    gu = GatherTn(u_all, u_send, u_recv)
    gt = GatherTn(t_all, t_send, t_recv)

    mine = slot_of(xh, yy, core)
    theirs = slot_of(d // (2 * NY), lax.rem(d // 2, NY), lax.rem(d, 2))
    loads = []
    for number, (src, dst) in enumerate((
        (w_hbm, w_ref), (og_hbm.at[0], u_all.at[mine]), (q_hbm, q_ref), (k_hbm, k_ref),
        (v_hbm, v_ref), (m1_hbm, m1_ref), (m2_hbm, m2_ref),
    )):
        loads.append(pltpu.make_async_copy(src, dst, load_sem.at[number]))
        loads[-1].start()

    targets = [(dp_at(1 - xl, z), t), (d, tn_at(1 - xh, yy, core)), (d, tn_at(xh, yy, 1 - core))]
    for q in range(1, STEP_Z + 1):
        targets += [(dp_at(xl, z + q), t), (dp_at(xl, z - q), t)]
    for q in range(1, STEP_Y + 1):
        targets += [(d, tn_at(xh, yy + q, core)), (d, tn_at(xh, yy - q, core))]
    barrier = pltpu.get_barrier_semaphore()
    for target in targets:
        pl.semaphore_signal(barrier, inc=1, device_id=target, device_id_type=MESH)
    pl.semaphore_signal(barrier, inc=1, device_id=(t, d), device_id_type=MESH)

    loads[0].wait()
    w_all[d] = w_ref[...].astype(BF16)
    loads[1].wait()
    start = start_ref[0]

    def lanes(rows):
        return lax.broadcasted_iota(jnp.int32, (rows, 128), 1)

    def sublanes(rows):
        return lax.broadcasted_iota(jnp.int32, (rows, 128), 0)

    def visible(jb, rows, first):
        return jb * 128 + lanes(rows) <= start + (first + sublanes(rows))

    def shifted(prev, cur, nxt, by):
        if by == 0:
            return cur
        lane = lanes(cur.shape[0])
        if by > 0:
            return pltpu.roll(jnp.where(lane >= by, cur, nxt), 128 - by, 1)
        return pltpu.roll(jnp.where(lane < 128 + by, cur, prev), -by, 1)

    def score_block(jb, carry):
        keys = k_ref[0, pl.ds(pl.multiple_of(jb * 128, 128), 128), :]
        raw = dot_cols(qp[...], keys) * scale
        xp[jb + 1] = jnp.where(visible(jb, xp.shape[1], -HALF), raw, 0.0)
        return carry

    def row_sums(src, jb, first, rows, flip):
        prev = src[jb, pl.ds(first, rows), :]
        cur = src[jb + 1, pl.ds(first, rows), :]
        nxt = src[jb + 2, pl.ds(first, rows), :]
        groups = (range(0, 3), range(3, CR)) if rows > 40 else (range(CR),)
        sums = [None] * CR
        for group in groups:
            for b in range(CC):
                moved = shifted(prev, cur, nxt, (HALF - b) if flip else (b - HALF))
                moved = moved.reshape(rows // 8, 8, 128)
                for a in group:
                    term = taps[a * CC + b][None] * moved
                    sums[a] = term if b == 0 else sums[a] + term
        return [total.reshape(rows, 128) for total in sums]

    def mix_half(tile, half):
        first = tile * WIDE
        rows = WIDE + 8

        def mix(jb, carry):
            sums = row_sums(xp, jb, first, rows, False)
            total = sums[CR - 1]
            for a in range(CR - 1):
                total = total + pltpu.roll(sums[a], rows - (HALF - a), 0)
            total = jnp.where(visible(jb, WIDE, first), total[:WIDE], -jnp.inf)
            prob[jb, pl.ds(first, WIDE), :] = total
            return carry

        lax.fori_loop(half * blocks // 2, (half + 1) * blocks // 2, mix, 0)

    def weights(tile):
        first = tile * WIDE
        span = pl.ds(first, WIDE)
        top = prob[0, span, :]
        for jb in range(1, blocks):
            top = jnp.maximum(top, prob[jb, span, :])
        top = jnp.max(top, axis=1, keepdims=True)
        total = jnp.zeros((WIDE, 128), F32)
        for jb in range(blocks):
            term = jnp.exp(prob[jb, span, :] - top)
            prob[jb, span, :] = term
            total = total + term
        inverse = 1.0 / jnp.sum(total, axis=1, keepdims=True)
        out = jnp.zeros((WIDE, 128), F32)
        for jb in range(blocks):
            weight = prob[jb, span, :] * inverse
            prob[jb, span, :] = weight
            rounded = weight.astype(BF16)
            prob_bf[jb, span, :] = rounded
            out = out + dot_mid(rounded, v_ref[0, pl.ds(jb * 128, 128), :])
        o_own[span, :] = out

    def prepare():
        qp[pl.ds(128, 16), :] = jnp.zeros((16, 128), BF16)
        loads[2].wait()
        qp[pl.ds(0, q_ref.shape[1]), :] = q_ref[0]
        loads[3].wait()
        for edge in (0, blocks + 1):
            xp[edge] = jnp.zeros((xp.shape[1], 128), F32)
            dcp[edge] = jnp.zeros((dcp.shape[1], 128), F32)
        for inner in range(1, blocks + 1):
            dcp[inner, pl.ds(0, 8), :] = jnp.zeros((8, 128), F32)
            dcp[inner, pl.ds(136, 16), :] = jnp.zeros((16, 128), F32)
        for a in range(CR):
            for b in range(CC):
                taps[a * CC + b] = jnp.full((8, 128), tap_ref[a, 0, b], F32)
        acc[...] = jnp.zeros(acc.shape, F32)
        loads[4].wait()

    def forward_part(part):
        if part == 0:
            prepare()
            lax.fori_loop(0, blocks, score_block, 0)
        mix_half(part // 2, part % 2)
        if part % 2 == 1:
            weights(part // 2)
        if part == 3:
            o_all[d] = jnp.transpose(o_own[...].astype(BF16))

    ahead = z < NZ // 2

    @pl.when(ahead)
    def _():
        for part in range(4):
            forward_part(part)

    pl.semaphore_wait(barrier, len(targets) + 1)

    gw.begin()
    gu.begin()

    transpose = pltpu.make_async_remote_copy(
        src_ref=u_all.at[mine], dst_ref=t_all.at[theirs],
        send_sem=p_send.at[0], recv_sem=p_send.at[1],
        device_id=(t, d), device_id_type=MESH,
    )

    @pl.when(d != t)
    def _():
        transpose.start()

    @pl.when(d == t)
    def _():
        t_all[mine] = u_all[mine]

    def late(part):
        @pl.when(jnp.logical_not(ahead))
        def _():
            forward_part(part)

    late(0)
    gu.crossed()
    gw.stage(0)
    late(1)
    gw.stage(1)
    gu.both(0)
    late(2)
    gw.stage(2)
    gu.both(1)
    late(3)
    go.begin()
    gw.stage(3)
    gu.both(2)

    @pl.when(d != t)
    def _():
        landed(t_all.at[mine], p_send.at[0], p_send.at[1]).wait_recv()

    gt.begin()
    gu.both(3)
    gu.finish()
    gw.finish()

    grad_out = jnp.zeros((128, 128), F32)
    for c in range(dp_count // 2):
        left = jnp.concatenate([u_all[c], u_all[2 * NY + c]], axis=1)
        right = jnp.concatenate([w_all[2 * c], w_all[2 * c + 1]], axis=1)
        grad_out = grad_out + dot_cols(left, right)
    do_bf[...] = grad_out.astype(BF16)

    inner = jnp.zeros((128, 128), F32)
    for jb in range(blocks):
        part = dot_cols(do_bf[...], v_ref[0, pl.ds(jb * 128, 128), :])
        dpp[jb] = part
        inner = inner + prob[jb] * part
    inner = jnp.sum(inner, axis=1, keepdims=True)
    for jb in range(blocks):
        dcp[jb + 1, pl.ds(8, 128), :] = prob[jb] * (dpp[jb] - inner)
    go.stage(0)
    gt.crossed()
    gt.both(0)

    def tap_grads(tile):
        first = tile * TILE
        rows = TILE + 8

        def body(jb, carry):
            wide = xp[jb + 1, pl.ds(first, rows), :]
            scores = []
            for a in range(CR):
                turned = wide if a == CR - 1 else pltpu.roll(wide, rows - (HALF - a), 0)
                scores.append(turned[:TILE].reshape(TILE // 8, 8, 128))
            prev = dcp[jb, pl.ds(8 + first, TILE), :]
            cur = dcp[jb + 1, pl.ds(8 + first, TILE), :]
            nxt = dcp[jb + 2, pl.ds(8 + first, TILE), :]
            for b in range(CC):
                moved = shifted(prev, cur, nxt, HALF - b).reshape(TILE // 8, 8, 128)
                for a in range(CR):
                    acc[a * 16 + b] += jnp.sum(scores[a] * moved, axis=0)
            return carry

        lax.fori_loop(0, blocks, body, 0)

    def grad_tile(first, count):
        rows = count + 8

        def body(jb, carry):
            sums = row_sums(dcp, jb, first, rows, True)
            total = None
            for a in range(CR):
                turned = pltpu.roll(sums[a], rows - (3 + a), 0)[:count]
                total = turned if total is None else total + turned
            total = jnp.where(visible(jb, count, first - HALF), total, 0.0)
            ds[jb, pl.ds(first, count), :] = total.astype(BF16)
            return carry

        lax.fori_loop(0, blocks, body, 0)

    tap_grads(0)
    tap_grads(1)
    go.stage(1)
    gt.both(1)
    tap_grads(2)
    tap_grads(3)

    folded = jnp.sum(acc[...], axis=1)
    kg_row = lax.dot_general(
        jnp.ones((8, 128), F32), folded, (((1,), (1,)), ((), ())),
        preferred_element_type=F32, precision=lax.Precision.HIGHEST,
    )
    kg_all[d] = kg_row[0:1]
    go.stage(2)
    gt.both(2)
    for r in range(1, dp_count):
        push(kg_all.at[d], kg_sem.at[0], kg_sem.at[1], (lax.rem(d + r, dp_count), t))

    grad_tile(0, WIDE)
    go.stage(3)
    gt.both(3)
    grad_tile(WIDE, WIDE)
    grad_tile(2 * WIDE, 16)

    grad_query = jnp.zeros((qp.shape[0], 128), F32)
    for jb in range(blocks):
        span = pl.ds(jb * 128, 128)
        grad_query = grad_query + dot_mid(ds[jb], k_ref[0, span, :])
        dk_ref[0, span, :] = (scale * dot_rows(ds[jb], qp[...])).astype(BF16)
        dv_ref[0, span, :] = dot_rows(prob_bf[jb], do_bf[...]).astype(BF16)
    dq_ref[0] = (scale * grad_query[: q_ref.shape[1]]).astype(BF16)

    gt.finish()
    go.finish()
    total = jnp.zeros((128, 128), F32)
    for g in range(dp_count // 2):
        left = jnp.concatenate([o_all[2 * g], o_all[2 * g + 1]], axis=1)
        right = jnp.concatenate([t_all[g], t_all[2 * NY + g]], axis=0)
        total = total + dot_mid(left, right)
    loads[5].wait()
    loads[6].wait()
    grad = total * (1.0 / dp_count)
    one = beta_one * m1_ref[...] + (1.0 - beta_one) * grad
    two = beta_two * m2_ref[...] + (1.0 - beta_two) * grad * grad
    m1n_ref[...] = one
    m2n_ref[...] = two
    wn_ref[...] = w_ref[...] - learn_rate * (
        (one / bias_one) / (jnp.sqrt(two / bias_two) + adam_eps) + decay_rate * w_ref[...]
    )

    others = landed(kg_all.at[pl.ds(0, dp_count - 1)], kg_sem.at[0], kg_sem.at[1])
    others.wait_recv()
    kg_sum = kg_all[0]
    for r in range(1, dp_count):
        kg_sum = kg_sum + kg_all[r]
    kg_sum = kg_sum * (1.0 / (dp_count * 128))
    for a in range(CR):
        row = kg_sum if a == 0 else pltpu.roll(kg_sum, 128 - 16 * a, 1)
        kg_ref[a] = row[:, :CC]

    others.wait_send()
    for gather in (gw, go, gu, gt):
        gather.drain()

    @pl.when(d != t)
    def _():
        transpose.wait_send()


def writer(*refs):
    count = len(refs) // 2
    copies = []
    for i in range(count):
        copies.append(pltpu.make_async_copy(refs[i], refs[count + i], refs[-1].at[i]))
        copies[-1].start()
    for copy in copies:
        copy.wait()


def shards(*args):
    args = list(args)
    queries, keys, proj = args[0], args[1], args[6]
    args[3] = jnp.transpose(args[3], (1, 0, 2))
    vmem = pl.BlockSpec(memory_space=pltpu.VMEM)
    smem = pl.BlockSpec(memory_space=pltpu.SMEM)
    hbm = pl.BlockSpec(memory_space=pltpu.HBM)
    dma = pltpu.SemaphoreType.DMA
    outs = (
        (queries.shape, BF16), (keys.shape, BF16), (keys.shape, BF16), (args[3].shape, F32),
        (proj.shape, F32), (proj.shape, F32), (proj.shape, F32),
    )
    gathered = pltpu.VMEM((32, 128, 128), BF16)
    blocks = keys.shape[1] // 128
    square = pltpu.VMEM(proj.shape, F32)
    held = pl.pallas_call(
        kernel,
        out_shape=[pltpu.VMEM(*out) for out in outs],
        in_specs=[hbm, hbm, hbm, smem, smem, hbm, hbm, hbm, hbm],
        out_specs=[vmem] * 7,
        scratch_shapes=[
            gathered, gathered, gathered, gathered,
            pltpu.VMEM((blocks + 2, 144, 128), F32),
            pltpu.VMEM((blocks, 128, 128), F32),
            pltpu.VMEM((blocks, 128, 128), BF16),
            pltpu.VMEM((blocks + 2, 152, 128), F32),
            pltpu.VMEM((blocks, 144, 128), BF16),
            pltpu.VMEM((144, 128), BF16),
            pltpu.VMEM((CR * CC, 8, 128), F32),
            pltpu.VMEM((128, 8, 128), F32),
            pltpu.VMEM((32, 1, 128), F32),
            pltpu.VMEM((blocks, 128, 128), F32),
            pltpu.VMEM((128, 128), BF16),
            pltpu.VMEM(queries.shape, BF16), pltpu.VMEM(keys.shape, BF16),
            pltpu.VMEM(keys.shape, BF16), square, square, square, square,
            dma((7,)),
            dma((1,)), dma((2 * NZ + 1,)), dma((1,)), dma((NZ + 1,)),
            dma((1,)), dma((2 * NY + 1,)), dma((1,)), dma((2 * NY + 1,)),
            dma((2,)), dma((2,)),
        ],
        compiler_params=pltpu.CompilerParams(
            collective_id=0, has_side_effects=True, vmem_limit_bytes=28 << 20
        ),
    )(*[arg if i in (3, 4) else pltpu.with_memory_space_constraint(arg, pltpu.HBM) for i, arg in enumerate(args)])
    held = [pltpu.with_memory_space_constraint(part, pltpu.VMEM) for part in held]
    final = list(pl.pallas_call(
        writer,
        out_shape=[pltpu.HBM(*out) for out in outs],
        in_specs=[vmem] * 7,
        out_specs=[hbm] * 7,
        scratch_shapes=[dma((7,))],
        compiler_params=pltpu.CompilerParams(vmem_limit_bytes=4 << 20),
    )(*held))
    final[3] = jnp.transpose(final[3], (1, 0, 2))
    return tuple(final)


def solution(mesh):
    heads = P("dp", None, "tensor")
    taps = P("tensor", None, None)
    grid = P("tensor", "dp")
    return jax.shard_map(
        shards,
        mesh=mesh,
        in_specs=(heads, heads, heads, taps, P("dp"), heads, grid, grid, grid),
        out_specs=(heads, heads, heads, taps, grid, grid, grid),
        check_vma=False,
    )
```

time: 82.9 us -> 70.2 us (0.85)
  the two profiles are of different devices: /device:TPU:28 before, /device:TPU:6 now
where the time goes in v2:
time: 70.2 us; the launch traced here: 70 us
  Pallas kernels  68.7 us (98%)
  between operations  1.31 us (2%)
    pallas_call x1, Pallas kernels, shards(): pl.pallas_call(kernel, out_shape=[pltpu.VMEM(*out) for out in outs], in_s...  67.8 us

profile of v2, /device:TPU:6, one launch (start us, length us, event | category | flops | bytes accessed | tf_op | source)
XLA Modules:
  0.0 70.0 jit_solution(15707353492930356659)
XLA Ops:
  0.6 0.0 copy-start
  1.3 0.0 copy-done
  1.3 67.8 %shard_map.144 = (bf16[1,133,128]{2,1,0:T(8,128)(2,1)S(1)}, bf16[1,1024,128]{2,1,0:T(8,128)(2,1)S(1)}, bf16[1,1024,128]{2,1,0:T(8,128)(2,1)S(1)}, f32[6,1,11]{2,...) custom-call(bf16[1,133,128]{2,1,0:T(8,128)(2,1)} %q_hbm.1, ...), custom_call_target="tpu_custom_call" | custom-call | tf_op jit(solution)/shard_map/pallas_call | solution.py:538
  69.1 0.9 %shard_map.145 = (bf16[1,133,128]{2,1,0:T(8,128)(2,1)}, bf16[1,1024,128]{2,1,0:T(8,128)(2,1)}, bf16[1,1024,128]{2,1,0:T(8,128)(2,1)}, f32[6,1,11]{2,1,0:T(1,128)...) custom-call(bf16[1,133,128]{2,1,0:T(8,128)(2,1)S(1)} %get-tuple-element.21.refs_0_, ...), custom_call_target="tpu_custom_call" | custom-call | tf_op jit(solution)/shard_map/pallas_call | solution.py:568
Async XLA Ops:
  0.6 0.7 copy-start

commit v3 on v2

--- a/solution.py
+++ b/solution.py
@@ -375,15 +375,14 @@
     late(3)
     go.begin()
     gw.stage(3)
-    gu.both(2)
 
     @pl.when(d != t)
     def _():
         landed(t_all.at[mine], p_send.at[0], p_send.at[1]).wait_recv()
 
     gt.begin()
-    gu.both(3)
     gu.finish()
+    go.stage(0)
     gw.finish()
 
     grad_out = jnp.zeros((128, 128), F32)
@@ -401,9 +400,8 @@
     inner = jnp.sum(inner, axis=1, keepdims=True)
     for jb in range(blocks):
         dcp[jb + 1, pl.ds(8, 128), :] = prob[jb] * (dpp[jb] - inner)
-    go.stage(0)
+    go.stage(1)
     gt.crossed()
-    gt.both(0)
 
     def tap_grads(tile):
         first = tile * TILE
@@ -443,9 +441,9 @@
 
     tap_grads(0)
     tap_grads(1)
-    go.stage(1)
-    gt.both(1)
+    gt.both(0)
     tap_grads(2)
+    go.stage(2)
     tap_grads(3)
 
     folded = jnp.sum(acc[...], axis=1)
@@ -454,14 +452,12 @@
         preferred_element_type=F32, precision=lax.Precision.HIGHEST,
     )
     kg_all[d] = kg_row[0:1]
-    go.stage(2)
-    gt.both(2)
     for r in range(1, dp_count):
         push(kg_all.at[d], kg_sem.at[0], kg_sem.at[1], (lax.rem(d + r, dp_count), t))
+    gt.both(1)
 
     grad_tile(0, WIDE)
     go.stage(3)
-    gt.both(3)
     grad_tile(WIDE, WIDE)
     grad_tile(2 * WIDE, 16)
 

time: 70.2 us -> 68.6 us (0.977)
  Pallas kernels: 68.7 us -> 66.4 us
    pallas_call x1, Pallas kernels: 67.8 us -> 65.5 us  [shards(): pl.pallas_call(kernel, out_shape=[pltpu.VMEM(*out) for out in outs], in_s...]
where the time goes in v3:
time: 68.6 us; the launch traced here: 67.7 us
  Pallas kernels  66.4 us (97%)
  between operations  1.31 us (2%)
    pallas_call x1, Pallas kernels, shards(): pl.pallas_call(kernel, out_shape=[pltpu.VMEM(*out) for out in outs], in_s...  65.5 us

profile of v3, /device:TPU:6, one launch (start us, length us, event | category | flops | bytes accessed | tf_op | source)
XLA Modules:
  0.0 67.7 jit_solution(1155054983560054865)
XLA Ops:
  0.6 0.0 copy-start
  1.3 0.0 copy-done
  1.3 65.5 %shard_map.144 = (bf16[1,133,128]{2,1,0:T(8,128)(2,1)S(1)}, bf16[1,1024,128]{2,1,0:T(8,128)(2,1)S(1)}, bf16[1,1024,128]{2,1,0:T(8,128)(2,1)S(1)}, f32[6,1,11]{2,...) custom-call(bf16[1,133,128]{2,1,0:T(8,128)(2,1)} %q_hbm.1, ...), custom_call_target="tpu_custom_call" | custom-call | tf_op jit(solution)/shard_map/pallas_call | solution.py:534
  66.8 0.9 %shard_map.145 = (bf16[1,133,128]{2,1,0:T(8,128)(2,1)}, bf16[1,1024,128]{2,1,0:T(8,128)(2,1)}, bf16[1,1024,128]{2,1,0:T(8,128)(2,1)}, f32[6,1,11]{2,1,0:T(1,128)...) custom-call(bf16[1,133,128]{2,1,0:T(8,128)(2,1)S(1)} %get-tuple-element.21.refs_0_, ...), custom_call_target="tpu_custom_call" | custom-call | tf_op jit(solution)/shard_map/pallas_call | solution.py:564
Async XLA Ops:
  0.6 0.7 %copy-start = (f32[1,6,11]{2,0,1:T(1,128)S(1)}, f32[1,6,11]{2,0,1:T(1,128)}, u32[]{:S(2)}) copy-start(f32[1,6,11]{2,0,1:T(1,128)} %param.12) | copy-start | bytes 796
